TPU v7x, 32 devices: a whole 2x2x4 slice. The times are simulated.
32 devices in a mesh: wide: 8 (over y, x, core), narrow: 4 (over z).
Axes of the slice: x: 2, y: 2, z: 4, core: 2. Of those that a mesh axis runs over, the one named last changes fastest.
Arguments:
- tokens: bfloat16 [4096, 1024], P(('wide', 'narrow')), may hold values from -6 to 6
- log_decay: float32 [8, 4096], P(None, 'wide'), as said below
- lengths: int32 [1], replicated, may hold values from 1024 to 4096, as said below
- pad_counts: int32 [1], replicated, may hold values from 0 to 255
- w_query: bfloat16 [1024, 1024], replicated, may hold values from -0.1875 to 0.1875
- w_key: bfloat16 [1024, 1024], replicated, may hold values from -0.1875 to 0.1875
- w_value: bfloat16 [1024, 1024], replicated, may hold values from -0.1875 to 0.1875
- w_gate: bfloat16 [1024, 1024], replicated, may hold values from -0.1875 to 0.1875
- w_out: bfloat16 [1024, 1024], replicated, may hold values from -0.375 to 0.375
- w_first: bfloat16 [1024, 2816], P(None, 'narrow'), may hold values from -0.1875 to 0.1875
- w_second: bfloat16 [1024, 2816], P(None, 'narrow'), may hold values from -0.1875 to 0.1875
- w_third: bfloat16 [2816, 1024], P('narrow'), may hold values from -0.109375 to 0.109375
- cotangent: bfloat16 [4096, 1024], P(('wide', 'narrow')), may hold values from -6 to 6
Outputs:
- output: bfloat16 [4096, 1024], P(('wide', 'narrow'))
- grad_tokens: float32 [4096, 1024], P(('wide', 'narrow'))
- grad_w_query: float32 [1024, 1024], replicated
- grad_w_key: float32 [1024, 1024], replicated
- grad_w_value: float32 [1024, 1024], replicated
- grad_w_gate: float32 [1024, 1024], replicated
- grad_w_out: float32 [1024, 1024], replicated
- grad_w_first: float32 [1024, 2816], P(None, 'narrow')
- grad_w_second: float32 [1024, 2816], P(None, 'narrow')
- grad_w_third: float32 [2816, 1024], P('narrow')
Inputs may be any that keep to these rules, and one draw needn't show every extreme that they name: `lengths`: multiples of 256 that sum to 4096; the longest is exactly 4096. `log_decay`: strictly negative.
All inputs are finite; a program needn't handle non-finite values.
Results may differ from a plain program's by a relative error of at most 0.017.
Values may be sent and summed in bfloat16 or wider, within the bound.
No kernel may reach another device: no remote copies, remote signals or barrier semaphores. Data moves between devices by JAX's collectives and lax.ppermute only.
A program may use at most 192 MiB of HBM per device.

v0:
```python
import jax
import jax.numpy as jnp
from jax import lax
from jax.sharding import PartitionSpec as P

BLOCK = 256
LONGEST = 8192
epsilon = 1e-06
precise = lax.Precision.HIGHEST


def from_behind(block, axis, distance):
    devices = range(lax.axis_size(axis))
    route = [(i - distance, i) for i in devices if i - distance in devices]
    return lax.ppermute(block, axis, route)


def rms_norm(values):
    return values * lax.rsqrt(jnp.mean(values * values, axis=-1, keepdims=True) + epsilon)


def rms_back(values, gradient):
    inverse_rms = lax.rsqrt(jnp.mean(values * values, axis=-1, keepdims=True) + epsilon)
    normed = values * inverse_rms
    return inverse_rms * (gradient - normed * jnp.mean(gradient * normed, axis=-1, keepdims=True))


def silu_slope(values):
    squashed = jax.nn.sigmoid(values)
    return squashed * (1.0 + values * (1.0 - squashed))


def token_layout(lengths, pad_counts, anchor, total_rows):
    ends = jnp.cumsum(lengths, dtype=jnp.int32)
    starts = ends - lengths
    position = anchor + jnp.arange(total_rows, dtype=jnp.int32)
    inside = (position[:, None] >= starts[None, :]) & (position[:, None] < ends[None, :])
    limit = jnp.sum(jnp.where(inside, (ends - pad_counts)[None, :], 0), axis=1, dtype=jnp.int32)
    live = (position < limit).astype(jnp.float32)
    opening = jnp.any(position[:, None] == starts[None, :], axis=1).astype(jnp.float32)
    return (live, opening)


def project(left_hand, right_hand):
    return jnp.dot(left_hand, right_hand, preferred_element_type=jnp.float32)


def weight_grad(left_hand, right_hand):
    return jnp.einsum("tc,td->cd", left_hand, right_hand, preferred_element_type=jnp.float32)


def transposed(left_hand, right_hand):
    return jnp.einsum("td,cd->tc", left_hand, right_hand, preferred_element_type=jnp.float32)


def to_blocks(values, head_count, block_len):
    row_count, model_width = values.shape
    shaped = values.reshape(
        row_count // block_len, block_len, head_count, model_width // head_count
    )
    return shaped.transpose(0, 2, 1, 3)


def from_blocks(values):
    block_count, head_count, block_len, head_size = values.shape
    return values.transpose(0, 2, 1, 3).reshape(block_count * block_len, head_count * head_size)


def body(
    tokens,
    log_decay,
    lengths,
    pad_counts,
    w_query,
    w_key,
    w_value,
    w_gate,
    w_out,
    w_first,
    w_second,
    w_third,
    cotangent,
):
    head_count = log_decay.shape[0]
    local_rows = log_decay.shape[1]
    share_rows = tokens.shape[0]
    block_len = BLOCK
    block_count = local_rows // block_len
    own_start = lax.axis_index("narrow") * share_rows
    live, opening = token_layout(
        lengths, pad_counts, lax.axis_index("wide") * local_rows, local_rows
    )
    keep_block = 1.0 - opening.reshape(block_count, block_len)[:, 0]
    whole_rows = lax.all_gather(tokens, "narrow", axis=0, tiled=True)
    normed_one = rms_norm(whole_rows.astype(jnp.float32)).astype(jnp.bfloat16)
    query_lin = project(normed_one, w_query)
    key_lin = project(normed_one, w_key)
    value_lin = project(normed_one, w_value)
    gate_act = jax.nn.sigmoid(project(normed_one, w_gate))
    query_blk = to_blocks(jax.nn.silu(query_lin).astype(jnp.bfloat16), head_count, block_len)
    key_blk = to_blocks(
        (jax.nn.silu(key_lin) * live[:, None]).astype(jnp.bfloat16), head_count, block_len
    )
    value_blk = to_blocks(value_lin.astype(jnp.bfloat16), head_count, block_len)
    cumulative = jnp.cumsum(
        log_decay.reshape(head_count, block_count, block_len), axis=2
    ).transpose(1, 0, 2)
    positions = jnp.arange(block_len, dtype=jnp.int32)
    causal = positions[:, None] >= positions[None, :]
    spread = cumulative[:, :, :, None] - cumulative[:, :, None, :]
    weights = jnp.where(causal, jnp.exp(jnp.where(causal, spread, 0.0)), 0.0)
    rise = jnp.exp(cumulative)
    tail = jnp.exp(cumulative[:, :, -1:] - cumulative)
    block_decay = jnp.exp(cumulative[:, :, -1]) * keep_block[:, None]
    query_float = query_blk.astype(jnp.float32)
    key_tail = key_blk.astype(jnp.float32) * tail[..., None]
    value_float = value_blk.astype(jnp.float32)
    contrib = jnp.einsum("bhsd,bhse->bhde", key_tail, value_float, precision=precise)

    def run_states(carry, inputs):
        decay_now, contrib_now = inputs
        return (decay_now[:, None, None] * carry + contrib_now, carry)

    zero_state = jnp.zeros(contrib.shape[1:], jnp.float32)
    local_final, local_enter = lax.scan(run_states, zero_state, (block_decay, contrib))
    factor_all = jnp.prod(block_decay, axis=0)
    ones_row = jnp.ones((1, head_count), jnp.float32)
    prefix = jnp.cumprod(jnp.concatenate([ones_row, block_decay[:-1]], axis=0), axis=0)
    after_factor = jnp.flip(
        jnp.cumprod(jnp.flip(jnp.concatenate([block_decay[1:], ones_row], axis=0), 0), axis=0), 0
    )
    hop_count = min(lax.axis_size("wide") - 1, LONGEST // local_rows + 1)

    def relay_step(step_index, incoming):
        return from_behind(factor_all[:, None, None] * incoming + local_final, "wide", 1)

    incoming = lax.fori_loop(0, hop_count, relay_step, zero_state)
    entering = local_enter + prefix[:, :, None, None] * incoming[None]
    kept_enter = entering * keep_block[:, None, None, None]
    raw_scores = jnp.einsum(
        "bhtd,bhsd->bhts", query_blk, key_blk, preferred_element_type=jnp.float32
    )
    scores = (raw_scores * weights).astype(jnp.bfloat16)
    intra = jnp.einsum("bhts,bhsd->bhtd", scores, value_blk, preferred_element_type=jnp.float32)
    query_rise = query_float * rise[..., None]
    inter = jnp.einsum("bhtd,bhde->bhte", query_rise, kept_enter, precision=precise)
    attended = from_blocks(intra + inter)
    attn_normed = rms_norm(attended)
    gated = (attn_normed * gate_act).astype(jnp.bfloat16)
    gated_own = lax.dynamic_slice_in_dim(gated, own_start, share_rows, 0)
    hidden_state = tokens.astype(jnp.float32) + project(gated_own, w_out)
    normed_two = rms_norm(hidden_state).astype(jnp.bfloat16)
    gathered_two = lax.all_gather(normed_two, "narrow", axis=0, tiled=True)
    first_lin = project(gathered_two, w_first)
    second_lin = project(gathered_two, w_second)
    product = (first_lin * second_lin).astype(jnp.bfloat16)
    ffn_own = lax.psum_scatter(
        project(product, w_third).astype(jnp.bfloat16), "narrow", scatter_dimension=0, tiled=True
    ).astype(jnp.float32)
    output = (hidden_state + ffn_own).astype(jnp.bfloat16)
    grad_whole = lax.all_gather(cotangent, "narrow", axis=0, tiled=True)
    grad_w_third = weight_grad(product, grad_whole)
    grad_product = transposed(grad_whole, w_third)
    grad_first = (grad_product * second_lin).astype(jnp.bfloat16)
    grad_second = (grad_product * first_lin).astype(jnp.bfloat16)
    grad_w_first = weight_grad(gathered_two, grad_first)
    grad_w_second = weight_grad(gathered_two, grad_second)
    grad_normed_two = lax.psum_scatter(
        transposed(grad_first, w_first) + transposed(grad_second, w_second),
        "narrow",
        scatter_dimension=0,
        tiled=True,
    )
    grad_hidden = cotangent.astype(jnp.float32) + rms_back(hidden_state, grad_normed_two)
    grad_hidden_low = grad_hidden.astype(jnp.bfloat16)
    grad_hidden_whole = lax.all_gather(grad_hidden_low, "narrow", axis=0, tiled=True)
    grad_gated = transposed(grad_hidden_whole, w_out)
    grad_gate_lin = (grad_gated * attn_normed * gate_act * (1.0 - gate_act)).astype(jnp.bfloat16)
    grad_attended = rms_back(attended, grad_gated * gate_act).astype(jnp.bfloat16)
    grad_blk = to_blocks(grad_attended, head_count, block_len)
    grad_float = grad_blk.astype(jnp.float32)
    grad_value = jnp.einsum("bhts,bhtd->bhsd", scores, grad_blk, preferred_element_type=jnp.float32)
    grad_raw = (
        jnp.einsum("bhtd,bhsd->bhts", grad_blk, value_blk, preferred_element_type=jnp.float32)
        * weights
    ).astype(jnp.bfloat16)
    grad_query = jnp.einsum(
        "bhts,bhsd->bhtd", grad_raw, key_blk, preferred_element_type=jnp.float32
    )
    grad_key = jnp.einsum(
        "bhts,bhtd->bhsd", grad_raw, query_blk, preferred_element_type=jnp.float32
    )
    grad_query = grad_query + rise[..., None] * jnp.einsum(
        "bhte,bhde->bhtd", grad_float, kept_enter, precision=precise
    )
    enter_direct = keep_block[:, None, None, None] * jnp.einsum(
        "bhtd,bhte->bhde", query_rise, grad_float, precision=precise
    )

    def back_states(carry, inputs):
        decay_now, direct_now = inputs
        return (direct_now + decay_now[:, None, None] * carry, carry)

    local_first, local_after = lax.scan(
        back_states, zero_state, (block_decay, enter_direct), reverse=True
    )
    hop_count = min(lax.axis_size("wide") - 1, LONGEST // local_rows + 1)

    def relay_back(step_index, arriving):
        return from_behind(
            (factor_all[:, None, None] * arriving + local_first).astype(jnp.bfloat16), "wide", -1
        ).astype(jnp.float32)

    arriving = lax.fori_loop(0, hop_count, relay_back, zero_state)
    grad_contrib = local_after + after_factor[:, :, None, None] * arriving[None]
    grad_key = grad_key + tail[..., None] * jnp.einsum(
        "bhse,bhde->bhsd", value_float, grad_contrib, precision=precise
    )
    grad_value = grad_value + jnp.einsum(
        "bhsd,bhde->bhse", key_tail, grad_contrib, precision=precise
    )
    grad_query_lin = (from_blocks(grad_query) * silu_slope(query_lin)).astype(jnp.bfloat16)
    grad_key_lin = (from_blocks(grad_key) * live[:, None] * silu_slope(key_lin)).astype(
        jnp.bfloat16
    )
    grad_value_lin = from_blocks(grad_value).astype(jnp.bfloat16)
    grad_normed_one = (
        transposed(grad_query_lin, w_query)
        + transposed(grad_key_lin, w_key)
        + transposed(grad_value_lin, w_value)
        + transposed(grad_gate_lin, w_gate)
    )
    grad_own = lax.dynamic_slice_in_dim(grad_normed_one, own_start, share_rows, 0)
    grad_tokens = grad_hidden + rms_back(tokens.astype(jnp.float32), grad_own)
    summed = (
        lax.psum(weight_grad(normed_one, grad_query_lin).astype(jnp.bfloat16), "wide").astype(
            jnp.float32
        ),
        lax.psum(weight_grad(normed_one, grad_key_lin).astype(jnp.bfloat16), "wide").astype(
            jnp.float32
        ),
        lax.psum(weight_grad(normed_one, grad_value_lin).astype(jnp.bfloat16), "wide").astype(
            jnp.float32
        ),
        lax.psum(weight_grad(normed_one, grad_gate_lin).astype(jnp.bfloat16), "wide").astype(
            jnp.float32
        ),
        lax.psum(weight_grad(gated, grad_hidden_whole).astype(jnp.bfloat16), "wide").astype(
            jnp.float32
        ),
        lax.psum(grad_w_first.astype(jnp.bfloat16), "wide").astype(jnp.float32),
        lax.psum(grad_w_second.astype(jnp.bfloat16), "wide").astype(jnp.float32),
        lax.psum(grad_w_third.astype(jnp.bfloat16), "wide").astype(jnp.float32),
    )
    mixer_total = summed[:5]
    glu_total = summed[5:]
    return (
        output,
        grad_tokens,
        mixer_total[0],
        mixer_total[1],
        mixer_total[2],
        mixer_total[3],
        mixer_total[4],
        glu_total[0],
        glu_total[1],
        glu_total[2],
    )


def solution(mesh):
    in_specs = (
        P(("wide", "narrow"), None),
        P(None, "wide"),
        P(),
        P(),
        P(),
        P(),
        P(),
        P(),
        P(),
        P(None, "narrow"),
        P(None, "narrow"),
        P("narrow", None),
        P(("wide", "narrow"), None),
    )
    out_specs = (
        P(("wide", "narrow"), None),
        P(("wide", "narrow"), None),
        P(),
        P(),
        P(),
        P(),
        P(),
        P(None, "narrow"),
        P(None, "narrow"),
        P("narrow", None),
    )
    return jax.shard_map(body, mesh=mesh, in_specs=in_specs, out_specs=out_specs, check_vma=False)
```

profile of v0, /device:TPU:0, one launch (start us, length us, event | category | flops | bytes accessed | tf_op | source)
XLA Modules:
  0.0 669.6 jit_solution(619893740103989016)
XLA Ops:
  12.5 27.8 %all-gather.5.cloned.1.call-done = bf16[512,1024]{1,0:T(8,128)(2,1)} async-done(((bf16[128,1024]{1,0:T(8,128)(2,1)}), bf16[512,1024]{1,0:T(8,128)(2,1)}) %all-gather.5.cloned.1.call-update) | async-done | bytes 1048592 | tf_op jit(solution)/shard_map/all_gather | solution.py:94
  41.8 3.2 fusion.96
  48.4 2.4 copy.127
  50.8 3.2 fusion.94
  59.9 3.5 fusion.12
  64.6 4.0 while.52
  68.6 2.4 copy.107
  71.0 3.1 multiply_convert_fusion.1
  76.3 73.5 %while.51 = (s32[]{:T(128)}, f32[8,128,128]{2,1,0:T(8,128)S(1)}, f32[8]{0:T(128)S(1)}, f32[8,128,128]{2,1,0:T(8,128)S(1)}, s32[]{:T(128)}) while((s32[]{:T(128)}, f32[8,128,128]{2,1,0:T(8,128)S(1)}, f32[8]{0:T(128)S(1)}, f32[8,128,128]{2,1,0:T(8,128)S(1)}, s32[]{:T(128)}) %tuple.105), condition=%wide.region_8.9_spmd, body=%wide.region_7.8_spmd.sunk | while | flops 262146 | bytes 3670149 | solution.py:137
  81.2 8.8 %collective-permute-start = (f32[8,128,128]{2,1,0:T(8,128)}, f32[8,128,128]{2,1,0:T(8,128)S(1)}, u32[]{:S(2)}, u32[]{:S(2)}) collective-permute-start(f32[8,128,128]{2,1,0:T(8,128)} %multiply_add_fusion.6), channel_id=1, source_target_pairs={{0,4},{4,8},{8,12},{12,16},{16,20},{20,24},{24,28},{1,5},{5,9},{9,... | collective-permute-start | bytes 1572872 | tf_op jit(solution)/shard_map/while/body/eval_jaxpr/ppermute | solution.py:15
  92.6 9.0 %collective-permute-start = (f32[8,128,128]{2,1,0:T(8,128)}, f32[8,128,128]{2,1,0:T(8,128)S(1)}, u32[]{:S(2)}, u32[]{:S(2)}) collective-permute-start(f32[8,128,128]{2,1,0:T(8,128)} %multiply_add_fusion.6), channel_id=1, source_target_pairs={{0,4},{4,8},{8,12},{12,16},{16,20},{20,24},{24,28},{1,5},{5,9},{9,... | collective-permute-start | bytes 1572872 | tf_op jit(solution)/shard_map/while/body/eval_jaxpr/ppermute | solution.py:15
  104.2 9.0 %collective-permute-start = (f32[8,128,128]{2,1,0:T(8,128)}, f32[8,128,128]{2,1,0:T(8,128)S(1)}, u32[]{:S(2)}, u32[]{:S(2)}) collective-permute-start(f32[8,128,128]{2,1,0:T(8,128)} %multiply_add_fusion.6), channel_id=1, source_target_pairs={{0,4},{4,8},{8,12},{12,16},{16,20},{20,24},{24,28},{1,5},{5,9},{9,... | collective-permute-start | bytes 1572872 | tf_op jit(solution)/shard_map/while/body/eval_jaxpr/ppermute | solution.py:15
  115.8 9.0 %collective-permute-start = (f32[8,128,128]{2,1,0:T(8,128)}, f32[8,128,128]{2,1,0:T(8,128)S(1)}, u32[]{:S(2)}, u32[]{:S(2)}) collective-permute-start(f32[8,128,128]{2,1,0:T(8,128)} %multiply_add_fusion.6), channel_id=1, source_target_pairs={{0,4},{4,8},{8,12},{12,16},{16,20},{20,24},{24,28},{1,5},{5,9},{9,... | collective-permute-start | bytes 1572872 | tf_op jit(solution)/shard_map/while/body/eval_jaxpr/ppermute | solution.py:15
  127.4 9.0 %collective-permute-start = (f32[8,128,128]{2,1,0:T(8,128)}, f32[8,128,128]{2,1,0:T(8,128)S(1)}, u32[]{:S(2)}, u32[]{:S(2)}) collective-permute-start(f32[8,128,128]{2,1,0:T(8,128)} %multiply_add_fusion.6), channel_id=1, source_target_pairs={{0,4},{4,8},{8,12},{12,16},{16,20},{20,24},{24,28},{1,5},{5,9},{9,... | collective-permute-start | bytes 1572872 | tf_op jit(solution)/shard_map/while/body/eval_jaxpr/ppermute | solution.py:15
  139.0 9.0 %collective-permute-start = (f32[8,128,128]{2,1,0:T(8,128)}, f32[8,128,128]{2,1,0:T(8,128)S(1)}, u32[]{:S(2)}, u32[]{:S(2)}) collective-permute-start(f32[8,128,128]{2,1,0:T(8,128)} %multiply_add_fusion.6), channel_id=1, source_target_pairs={{0,4},{4,8},{8,12},{12,16},{16,20},{20,24},{24,28},{1,5},{5,9},{9,... | collective-permute-start | bytes 1572872 | tf_op jit(solution)/shard_map/while/body/eval_jaxpr/ppermute | solution.py:15
  149.9 6.0 multiply_reduce_fusion.1
  155.9 2.9 copy.119
  158.9 5.0 multiply_convert_fusion.4
  166.6 40.0 %all-gather.7.cloned.1.call-done = bf16[512,1024]{1,0:T(8,128)(2,1)} async-done(((bf16[128,1024]{1,0:T(8,128)(2,1)}), bf16[512,1024]{1,0:T(8,128)(2,1)}) %all-gather.7.cloned.1.call-update) | async-done | bytes 1048592 | tf_op jit(solution)/shard_map/all_gather | solution.py:153
  206.6 3.9 fusion.100
  212.5 23.0 %all-gather.9.cloned.1.call-done = bf16[512,1024]{1,0:T(8,128)(2,1)} async-done(((bf16[128,1024]{1,0:T(8,128)(2,1)}), bf16[512,1024]{1,0:T(8,128)(2,1)}) %all-gather.9.cloned.1.call-update) | async-done | bytes 1048592 | tf_op jit(solution)/shard_map/all_gather | solution.py:161
  235.5 4.5 multiply_convert_fusion.7
  244.4 43.1 %reduce-scatter.5.cloned.1.call-done = f32[128,1024]{1,0:T(8,128)} async-done(((f32[512,1024]{1,0:T(8,128)}), f32[128,1024]{1,0:T(8,128)}) %reduce-scatter.5.cloned.1.call-update) | async-done | bytes 524304 | tf_op jit(solution)/shard_map/reduce_scatter | solution.py:168
  292.1 3.6 convolution_convert_fusion.8
  296.0 3.7 convolution_convert_fusion.6
  303.8 14.3 %all-gather.11.cloned.1.call-done = bf16[512,1024]{1,0:T(8,128)(2,1)} async-done(((bf16[128,1024]{1,0:T(8,128)(2,1)}), bf16[512,1024]{1,0:T(8,128)(2,1)}) %all-gather.11.cloned.1.call-update) | async-done | bytes 1048592 | tf_op jit(solution)/shard_map/all_gather | solution.py:176
  318.1 6.1 multiply_reduce_fusion
  335.2 4.0 while.53
  339.2 67.9 %while.54 = (s32[]{:T(128)}, f32[8,128,128]{2,1,0:T(8,128)}, f32[8]{0:T(128)S(1)}, f32[8,128,128]{2,1,0:T(8,128)S(1)}, s32[]{:T(128)}, /*index=5*/s32[]{:T(128)}) while((s32[]{:T(128)}, f32[8,128,128]{2,1,0:T(8,128)}, f32[8]{0:T(128)S(1)}, f32[8,128,128]{2,1,0:T(8,128)S(1)}, s32[]{:T(128)}, /*index=5*/s32[]{:T(128)}) %tuple.129), condition=%wide.region_20.21_spmd.clone, body=%wide.region_19.20_spmd.clone.sunk | while | flops 655363 | bytes 3145879 | solution.py:214
  347.7 5.6 collective-permute-done.1
  357.4 6.6 collective-permute-done.1
  368.0 6.6 collective-permute-done.1
  378.5 6.6 collective-permute-done.1
  389.1 6.6 collective-permute-done.1
  399.7 6.6 collective-permute-done.1
  407.2 4.1 fusion.11
  422.3 2.6 convolution_convert_fusion
  425.0 2.7 convolution_convert_fusion.4
  428.6 2.7 convolution_convert_fusion.3
  431.3 2.7 convolution_convert_fusion.2
  434.0 2.7 convolution_convert_fusion.1
  437.8 2.8 fusion.106
  449.5 193.0 %all-reduce.4.cloned.1.call-done = (bf16[1024,1024]{1,0:T(8,128)(2,1)}, bf16[1024,1024]{1,0:T(8,128)(2,1)}, bf16[1024,1024]{1,0:T(8,128)(2,1)}, bf16[1024,1024]{...) async-done(((bf16[1024,1024]{1,0:T(8,128)(2,1)}, ...) | async-done | bytes 14811152 | tf_op jit(solution)/shard_map/psum | solution.py:236
  642.5 4.2 convert_element_type.176
  646.8 2.5 convert_element_type.178
  649.2 2.5 convert_element_type.180
  651.7 2.5 convert_element_type.182
  654.2 2.5 convert_element_type.184
  (317 shorter events, 131.1 us)
Async XLA Ops:
  7.2 151.7 %copy-start = (bf16[1024,1024]{1,0:T(8,128)(2,1)S(1)}, bf16[1024,1024]{1,0:T(8,128)(2,1)}, u32[]{:S(2)}) copy-start(bf16[1024,1024]{1,0:T(8,128)(2,1)} %param.28) | copy-start | bytes 6291460
  7.2 33.1 %all-gather.5.cloned.1.call-start = ((), (), s32[]{:S(2)}) async-start(), calls=%async_computation.2 | async-start | bytes 1310720 | tf_op jit(solution)/shard_map/all_gather | solution.py:94
  7.9 198.6 %all-gather.7.cloned.1.call-start = ((), (), s32[]{:S(2)}) async-start(), calls=%async_computation.3 | async-start | bytes 1310720 | tf_op jit(solution)/shard_map/all_gather | solution.py:153
  10.1 35.0 %copy-start.59 = (f32[8,2,2]{0,1,2:T(2,128)}, f32[8,2,2]{0,1,2:T(2,128)S(1)}, u32[]{:S(2)}) copy-start(f32[8,2,2]{0,1,2:T(2,128)S(1)} %copy.112) | copy-start | bytes 388
  11.5 138.4 %copy-start.70 = (f32[2]{0:T(128)}, f32[2]{0:T(128)S(1)}, u32[]{:S(2)}) copy-start(f32[2]{0:T(128)S(1)} %fusion.84) | copy-start | bytes 28
  11.6 59.4 %copy-start.57 = (f32[2,8,256]{2,1,0:T(8,128)}, f32[2,8,256]{2,1,0:T(8,128)S(1)}, u32[]{:S(2)}) copy-start(f32[2,8,256]{2,1,0:T(8,128)S(1)} %bitcast_bitcast_fusion.1) | copy-start | bytes 49156
  11.7 33.3 %copy-start.64 = (f32[2,8]{1,0:T(2,128)}, f32[2,8]{1,0:T(2,128)S(1)}, u32[]{:S(2)}) copy-start(f32[2,8]{1,0:T(2,128)S(1)} %slice_reduce_fusion) | copy-start | bytes 196
  12.4 137.5 %copy-start.65 = (f32[2,8]{1,0:T(2,128)}, f32[2,8]{1,0:T(2,128)S(1)}, u32[]{:S(2)}) copy-start(f32[2,8]{1,0:T(2,128)S(1)} %reduce_window.14) | copy-start | bytes 196
  12.4 41.6 %copy-start.62 = (f32[512]{0:T(512)}, f32[512]{0:T(512)S(1)}, u32[]{:S(2)}) copy-start(f32[512]{0:T(512)S(1)} %fusion.81) | copy-start | bytes 6148
  41.8 117.0 %copy-start.74 = (f32[512]{0:T(512)}, f32[512]{0:T(512)S(1)}, u32[]{:S(2)}) copy-start(f32[512]{0:T(512)S(1)} %add_rsqrt_fusion) | copy-start | bytes 6148
  58.8 4.6 copy-start.10
  68.6 5.5 copy-start.72
  77.2 3.0 collective-permute-start
  81.2 10.5 %collective-permute-start = (f32[8,128,128]{2,1,0:T(8,128)}, f32[8,128,128]{2,1,0:T(8,128)S(1)}, u32[]{:S(2)}, u32[]{:S(2)}) collective-permute-start(f32[8,128,128]{2,1,0:T(8,128)} %multiply_add_fusion.6), channel_id=1, source_target_pairs={{0,4},{4,8},{8,12},{12,16},{16,20},{20,24},{24,28},{1,5},{5,9},{9,... | collective-permute-start | bytes 1572872 | tf_op jit(solution)/shard_map/while/body/eval_jaxpr/ppermute | solution.py:15
  92.6 10.7 %collective-permute-start = (f32[8,128,128]{2,1,0:T(8,128)}, f32[8,128,128]{2,1,0:T(8,128)S(1)}, u32[]{:S(2)}, u32[]{:S(2)}) collective-permute-start(f32[8,128,128]{2,1,0:T(8,128)} %multiply_add_fusion.6), channel_id=1, source_target_pairs={{0,4},{4,8},{8,12},{12,16},{16,20},{20,24},{24,28},{1,5},{5,9},{9,... | collective-permute-start | bytes 1572872 | tf_op jit(solution)/shard_map/while/body/eval_jaxpr/ppermute | solution.py:15
  104.2 10.7 %collective-permute-start = (f32[8,128,128]{2,1,0:T(8,128)}, f32[8,128,128]{2,1,0:T(8,128)S(1)}, u32[]{:S(2)}, u32[]{:S(2)}) collective-permute-start(f32[8,128,128]{2,1,0:T(8,128)} %multiply_add_fusion.6), channel_id=1, source_target_pairs={{0,4},{4,8},{8,12},{12,16},{16,20},{20,24},{24,28},{1,5},{5,9},{9,... | collective-permute-start | bytes 1572872 | tf_op jit(solution)/shard_map/while/body/eval_jaxpr/ppermute | solution.py:15
  115.8 10.7 %collective-permute-start = (f32[8,128,128]{2,1,0:T(8,128)}, f32[8,128,128]{2,1,0:T(8,128)S(1)}, u32[]{:S(2)}, u32[]{:S(2)}) collective-permute-start(f32[8,128,128]{2,1,0:T(8,128)} %multiply_add_fusion.6), channel_id=1, source_target_pairs={{0,4},{4,8},{8,12},{12,16},{16,20},{20,24},{24,28},{1,5},{5,9},{9,... | collective-permute-start | bytes 1572872 | tf_op jit(solution)/shard_map/while/body/eval_jaxpr/ppermute | solution.py:15
  127.4 10.7 %collective-permute-start = (f32[8,128,128]{2,1,0:T(8,128)}, f32[8,128,128]{2,1,0:T(8,128)S(1)}, u32[]{:S(2)}, u32[]{:S(2)}) collective-permute-start(f32[8,128,128]{2,1,0:T(8,128)} %multiply_add_fusion.6), channel_id=1, source_target_pairs={{0,4},{4,8},{8,12},{12,16},{16,20},{20,24},{24,28},{1,5},{5,9},{9,... | collective-permute-start | bytes 1572872 | tf_op jit(solution)/shard_map/while/body/eval_jaxpr/ppermute | solution.py:15
  139.0 10.7 %collective-permute-start = (f32[8,128,128]{2,1,0:T(8,128)}, f32[8,128,128]{2,1,0:T(8,128)S(1)}, u32[]{:S(2)}, u32[]{:S(2)}) collective-permute-start(f32[8,128,128]{2,1,0:T(8,128)} %multiply_add_fusion.6), channel_id=1, source_target_pairs={{0,4},{4,8},{8,12},{12,16},{16,20},{20,24},{24,28},{1,5},{5,9},{9,... | collective-permute-start | bytes 1572872 | tf_op jit(solution)/shard_map/while/body/eval_jaxpr/ppermute | solution.py:15
  149.9 6.1 copy-start.55
  158.8 5.1 copy-start.60
  158.9 5.1 copy-start.16
  158.9 5.1 copy-start.25
  164.9 123.8 %copy-start.5 = (f32[128,1024]{1,0:T(8,128)}, f32[128,1024]{1,0:T(8,128)S(1)}, u32[]{:S(2)}) copy-start(f32[128,1024]{1,0:T(8,128)S(1)} %get-tuple-element.310) | copy-start | bytes 1572868
  164.9 123.8 %copy-start.68 = (f32[128]{0:T(128)}, f32[128]{0:T(128)S(1)}, u32[]{:S(2)}) copy-start(f32[128]{0:T(128)S(1)} %add_rsqrt_fusion.2) | copy-start | bytes 1540
  165.8 69.7 %all-gather.9.cloned.1.call-start = ((), (), s32[]{:S(2)}) async-start(), calls=%async_computation.5 | async-start | bytes 1310720 | tf_op jit(solution)/shard_map/all_gather | solution.py:161
  166.5 120.9 %reduce-scatter.5.cloned.1.call-start = ((), (), s32[]{:S(2)}) async-start(), calls=%async_computation.6 | async-start | bytes 2621440 | tf_op jit(solution)/shard_map/reduce_scatter | solution.py:168
  235.5 4.5 copy-start.83
  244.3 44.4 %copy-start.31 = (bf16[128,1024]{1,0:T(8,128)(2,1)S(1)}, bf16[128,1024]{1,0:T(8,128)(2,1)}, u32[]{:S(2)}) copy-start(bf16[128,1024]{1,0:T(8,128)(2,1)} %param.33) | copy-start | bytes 786436
  244.3 46.5 %copy-start.76 = (f32[1,8]{1,0:T(1,128)S(1)}, f32[1,8]{1,0:T(1,128)}, u32[]{:S(2)}) copy-start(f32[1,8]{1,0:T(1,128)} %get-tuple-element.303) | copy-start | bytes 100
  244.3 73.8 %all-gather.11.cloned.1.call-start = ((), (), s32[]{:S(2)}) async-start(), calls=%async_computation.7 | async-start | bytes 1310720 | tf_op jit(solution)/shard_map/all_gather | solution.py:176
  290.7 156.2 %reduce-scatter.3.cloned.1.call-start = ((), (), s32[]{:S(2)}) async-start(), calls=%async_computation.4 | async-start | bytes 1310720 | tf_op jit(solution)/shard_map/reduce_scatter | solution.py:157
  295.8 346.8 %all-reduce.4.cloned.1.call-start = ((), (), s32[]{:S(2)}) async-start(), calls=%async_computation.8 | async-start | bytes 29622272 | tf_op jit(solution)/shard_map/psum | solution.py:236
  301.7 16.3 %copy-start.61 = (f32[1,2,2,128]{3,1,2,0:T(2,128)S(1)}, f32[1,2,2,128]{3,1,2,0:T(2,128)}, u32[]{:S(2)}) copy-start(f32[1,2,2,128]{3,1,2,0:T(2,128)} %copy-done.60) | copy-start | bytes 6148
  318.1 6.1 copy-start.2
  325.0 5.0 copy-start.3
  339.2 67.9 %copy-start.67 = (f32[2,8]{1,0:T(2,128)S(1)}, f32[2,8]{1,0:T(2,128)}, u32[]{:S(2)}) copy-start(f32[2,8]{1,0:T(2,128)} %rev.8) | copy-start | bytes 196
  340.1 3.6 collective-permute-start.1
  346.4 6.9 %collective-permute-start.1 = (bf16[8,128,128]{2,1,0:T(8,128)(2,1)}, bf16[8,128,128]{2,1,0:T(8,128)(2,1)S(1)}, u32[]{:S(2)}, u32[]{:S(2)}) collective-permute-start(bf16[8,128,128]{2,1,0:T(8,128)(2,1)} %fusion.155), channel_id=1, source_target_pairs={{4,0},{8,4},{12,8},{16,12},{20,16},{24,20},{28,24},{5,1},{9,5},{13... | collective-permute-start | bytes 786440 | tf_op jit(solution)/shard_map/while/body/eval_jaxpr/ppermute | solution.py:15
  356.1 7.9 %collective-permute-start.1 = (bf16[8,128,128]{2,1,0:T(8,128)(2,1)}, bf16[8,128,128]{2,1,0:T(8,128)(2,1)S(1)}, u32[]{:S(2)}, u32[]{:S(2)}) collective-permute-start(bf16[8,128,128]{2,1,0:T(8,128)(2,1)} %fusion.155), channel_id=1, source_target_pairs={{4,0},{8,4},{12,8},{16,12},{20,16},{24,20},{28,24},{5,1},{9,5},{13... | collective-permute-start | bytes 786440 | tf_op jit(solution)/shard_map/while/body/eval_jaxpr/ppermute | solution.py:15
  366.7 7.9 %collective-permute-start.1 = (bf16[8,128,128]{2,1,0:T(8,128)(2,1)}, bf16[8,128,128]{2,1,0:T(8,128)(2,1)S(1)}, u32[]{:S(2)}, u32[]{:S(2)}) collective-permute-start(bf16[8,128,128]{2,1,0:T(8,128)(2,1)} %fusion.155), channel_id=1, source_target_pairs={{4,0},{8,4},{12,8},{16,12},{20,16},{24,20},{28,24},{5,1},{9,5},{13... | collective-permute-start | bytes 786440 | tf_op jit(solution)/shard_map/while/body/eval_jaxpr/ppermute | solution.py:15
  377.3 7.9 %collective-permute-start.1 = (bf16[8,128,128]{2,1,0:T(8,128)(2,1)}, bf16[8,128,128]{2,1,0:T(8,128)(2,1)S(1)}, u32[]{:S(2)}, u32[]{:S(2)}) collective-permute-start(bf16[8,128,128]{2,1,0:T(8,128)(2,1)} %fusion.155), channel_id=1, source_target_pairs={{4,0},{8,4},{12,8},{16,12},{20,16},{24,20},{28,24},{5,1},{9,5},{13... | collective-permute-start | bytes 786440 | tf_op jit(solution)/shard_map/while/body/eval_jaxpr/ppermute | solution.py:15
  387.9 7.9 %collective-permute-start.1 = (bf16[8,128,128]{2,1,0:T(8,128)(2,1)}, bf16[8,128,128]{2,1,0:T(8,128)(2,1)S(1)}, u32[]{:S(2)}, u32[]{:S(2)}) collective-permute-start(bf16[8,128,128]{2,1,0:T(8,128)(2,1)} %fusion.155), channel_id=1, source_target_pairs={{4,0},{8,4},{12,8},{16,12},{20,16},{24,20},{28,24},{5,1},{9,5},{13... | collective-permute-start | bytes 786440 | tf_op jit(solution)/shard_map/while/body/eval_jaxpr/ppermute | solution.py:15
  398.4 7.9 %collective-permute-start.1 = (bf16[8,128,128]{2,1,0:T(8,128)(2,1)}, bf16[8,128,128]{2,1,0:T(8,128)(2,1)S(1)}, u32[]{:S(2)}, u32[]{:S(2)}) collective-permute-start(bf16[8,128,128]{2,1,0:T(8,128)(2,1)} %fusion.155), channel_id=1, source_target_pairs={{4,0},{8,4},{12,8},{16,12},{20,16},{24,20},{28,24},{5,1},{9,5},{13... | collective-permute-start | bytes 786440 | tf_op jit(solution)/shard_map/while/body/eval_jaxpr/ppermute | solution.py:15
  407.2 4.1 copy-start.4
  407.2 4.1 copy-start.20
  412.9 18.4 %copy-start.51 = (bf16[2,256,8,128]{3,2,1,0:T(8,128)(2,1)}, bf16[2,256,8,128]{3,2,1,0:T(8,128)(2,1)S(1)}, u32[]{:S(2)}) copy-start(bf16[2,256,8,128]{3,2,1,0:T(8,128)(2,1)S(1)} %copy.126) | copy-start | bytes 3145732
  642.5 4.2 copy-start.35
  (61 other events, 128.6 us)
Sparse Core Ops, SparseCore 0:
  9.6 30.6 all-gather.4
  165.9 40.6 all-gather.6
  208.1 27.3 all-gather.8
  244.4 42.9 reduce-scatter.4
  290.8 27.2 all-gather.10
  320.2 26.6 reduce-scatter.2
  436.9 205.6 all-reduce.3
where the time goes:
time: 678 us; the launch traced here: 670 us
  waiting for transfers between devices  395 us (58%)
  matrix products  95.5 us (14%)
  other arithmetic  66.9 us (10%)
  starting transfers between devices  64.5 us (10%)
  local copies, waits for them, and re-layouts  30.2 us (4%)
  between operations  16.5 us (2%)
    psum x1, waiting for transfers between devices, body(): lax.psum(weight_grad(normed_one, grad_query_lin).astype(jnp.bfloat16), 'w...  193 us
    ppermute x14, starting transfers between devices, from_behind(): return lax.ppermute(block, axis, route)  64 us
    ppermute x14, waiting for transfers between devices, from_behind(): return lax.ppermute(block, axis, route)  52.8 us
    reduce_scatter x1, waiting for transfers between devices, body(): lax.psum_scatter(transposed(grad_first, w_first) + transposed(grad_second...  43.1 us
    all_gather x1, waiting for transfers between devices, body(): gathered_two = lax.all_gather(normed_two, 'narrow', axis=0, tiled=True)  40 us
    all_gather x1, waiting for transfers between devices, body(): whole_rows = lax.all_gather(tokens, 'narrow', axis=0, tiled=True)  27.8 us
    all_gather x1, waiting for transfers between devices, body(): grad_whole = lax.all_gather(cotangent, 'narrow', axis=0, tiled=True)  23 us
    dot_general x8, matrix products, project(): return jnp.dot(left_hand, right_hand, preferred_element_type=jnp.float32)  22.8 us
  transfers between devices with their start and end apart: 21, of which 20 were waited for; matrix products, arithmetic and copies ran while one was open for 14% of the time, Pallas kernels for 0%

commit v1 on v0

--- a/solution.py
+++ b/solution.py
@@ -233,9 +233,12 @@
     grad_own = lax.dynamic_slice_in_dim(grad_normed_one, own_start, share_rows, 0)
     grad_tokens = grad_hidden + rms_back(tokens.astype(jnp.float32), grad_own)
     summed = (
-        lax.psum(weight_grad(normed_one, grad_query_lin).astype(jnp.bfloat16), "wide").astype(
-            jnp.float32
-        ),
+        jnp.sum(
+            lax.all_gather(
+                weight_grad(normed_one, grad_query_lin).astype(jnp.bfloat16), axis_name="wide"
+            ),
+            0,
+        ).astype(jnp.float32),
         lax.psum(weight_grad(normed_one, grad_key_lin).astype(jnp.bfloat16), "wide").astype(
             jnp.float32
         ),

time: 678 us -> 735 us (1.084)
  waiting for transfers between devices: 395 us -> 436 us
  other arithmetic: 66.9 us -> 79.6 us
    all_gather x0 -> x1, waiting for transfers between devices: none -> 74.7 us  [body(): lax.all_gather(weight_grad(normed_one, grad_query_lin).astype(jnp.bfloat1...]
    psum x1, waiting for transfers between devices: 193 us -> 159 us  [body(): lax.psum(weight_grad(normed_one, grad_key_lin).astype(jnp.bfloat16), 'wide')]
    reduce_sum x0 -> x1, other arithmetic: none -> 10.8 us  [body(): jnp.sum(lax.all_gather(weight_grad(normed_one, grad_query_lin).astype(jnp...]
    unnamed x181 -> x179, local copies, waits for them, and re-layouts: 12.8 us -> 15.1 us
  transfers between devices with their start and end apart: 21 -> 22, of which waited for: 20 -> 21; matrix products, arithmetic and copies ran while one was open for 14% -> 16% of each run, Pallas kernels for 0% -> 0%
where the time goes in v1:
time: 735 us; the launch traced here: 726 us
  waiting for transfers between devices  436 us (59%)
  matrix products  96 us (13%)
  other arithmetic  79.6 us (11%)
  starting transfers between devices  64.7 us (9%)
  local copies, waits for them, and re-layouts  32.6 us (4%)
  between operations  16.5 us (2%)
    psum x1, waiting for transfers between devices, body(): lax.psum(weight_grad(normed_one, grad_key_lin).astype(jnp.bfloat16), 'wide')  159 us
    all_gather x1, waiting for transfers between devices, body(): lax.all_gather(weight_grad(normed_one, grad_query_lin).astype(jnp.bfloat1...  74.7 us
    ppermute x14, starting transfers between devices, from_behind(): return lax.ppermute(block, axis, route)  64 us
    ppermute x14, waiting for transfers between devices, from_behind(): return lax.ppermute(block, axis, route)  53 us
    reduce_scatter x1, waiting for transfers between devices, body(): lax.psum_scatter(transposed(grad_first, w_first) + transposed(grad_second...  43.1 us
    all_gather x1, waiting for transfers between devices, body(): gathered_two = lax.all_gather(normed_two, 'narrow', axis=0, tiled=True)  40 us
    all_gather x1, waiting for transfers between devices, body(): whole_rows = lax.all_gather(tokens, 'narrow', axis=0, tiled=True)  27.8 us
    all_gather x1, waiting for transfers between devices, body(): grad_whole = lax.all_gather(cotangent, 'narrow', axis=0, tiled=True)  23 us
  transfers between devices with their start and end apart: 22, of which 21 were waited for; matrix products, arithmetic and copies ran while one was open for 16% of the time, Pallas kernels for 0%

profile of v1, /device:TPU:0, one launch (start us, length us, event | category | flops | bytes accessed | tf_op | source)
XLA Modules:
  0.0 725.9 jit_solution(15662212976881553449)
XLA Ops:
  12.5 27.8 %all-gather.7.cloned.1.call-done = bf16[512,1024]{1,0:T(8,128)(2,1)} async-done(((bf16[128,1024]{1,0:T(8,128)(2,1)}), bf16[512,1024]{1,0:T(8,128)(2,1)}) %all-gather.7.cloned.1.call-update) | async-done | bytes 1048592 | tf_op jit(solution)/shard_map/all_gather | solution.py:94
  41.8 3.2 fusion.96
  50.8 3.2 fusion.94
  60.0 3.5 fusion.12
  64.6 4.1 while.52
  71.1 3.1 multiply_convert_fusion.1
  76.4 73.5 %while.51 = (s32[]{:T(128)}, f32[8,128,128]{2,1,0:T(8,128)S(1)}, f32[8]{0:T(128)S(1)}, f32[8,128,128]{2,1,0:T(8,128)S(1)}, s32[]{:T(128)}) while((s32[]{:T(128)}, f32[8,128,128]{2,1,0:T(8,128)S(1)}, f32[8]{0:T(128)S(1)}, f32[8,128,128]{2,1,0:T(8,128)S(1)}, s32[]{:T(128)}) %tuple.105), condition=%wide.region_8.9_spmd, body=%wide.region_7.8_spmd.sunk | while | flops 262146 | bytes 3670149 | solution.py:137
  81.3 8.8 %collective-permute-start = (f32[8,128,128]{2,1,0:T(8,128)}, f32[8,128,128]{2,1,0:T(8,128)S(1)}, u32[]{:S(2)}, u32[]{:S(2)}) collective-permute-start(f32[8,128,128]{2,1,0:T(8,128)} %multiply_add_fusion.6), channel_id=1, source_target_pairs={{0,4},{4,8},{8,12},{12,16},{16,20},{20,24},{24,28},{1,5},{5,9},{9,... | collective-permute-start | bytes 1572872 | tf_op jit(solution)/shard_map/while/body/eval_jaxpr/ppermute | solution.py:15
  92.7 9.0 %collective-permute-start = (f32[8,128,128]{2,1,0:T(8,128)}, f32[8,128,128]{2,1,0:T(8,128)S(1)}, u32[]{:S(2)}, u32[]{:S(2)}) collective-permute-start(f32[8,128,128]{2,1,0:T(8,128)} %multiply_add_fusion.6), channel_id=1, source_target_pairs={{0,4},{4,8},{8,12},{12,16},{16,20},{20,24},{24,28},{1,5},{5,9},{9,... | collective-permute-start | bytes 1572872 | tf_op jit(solution)/shard_map/while/body/eval_jaxpr/ppermute | solution.py:15
  104.3 9.0 %collective-permute-start = (f32[8,128,128]{2,1,0:T(8,128)}, f32[8,128,128]{2,1,0:T(8,128)S(1)}, u32[]{:S(2)}, u32[]{:S(2)}) collective-permute-start(f32[8,128,128]{2,1,0:T(8,128)} %multiply_add_fusion.6), channel_id=1, source_target_pairs={{0,4},{4,8},{8,12},{12,16},{16,20},{20,24},{24,28},{1,5},{5,9},{9,... | collective-permute-start | bytes 1572872 | tf_op jit(solution)/shard_map/while/body/eval_jaxpr/ppermute | solution.py:15
  115.9 9.0 %collective-permute-start = (f32[8,128,128]{2,1,0:T(8,128)}, f32[8,128,128]{2,1,0:T(8,128)S(1)}, u32[]{:S(2)}, u32[]{:S(2)}) collective-permute-start(f32[8,128,128]{2,1,0:T(8,128)} %multiply_add_fusion.6), channel_id=1, source_target_pairs={{0,4},{4,8},{8,12},{12,16},{16,20},{20,24},{24,28},{1,5},{5,9},{9,... | collective-permute-start | bytes 1572872 | tf_op jit(solution)/shard_map/while/body/eval_jaxpr/ppermute | solution.py:15
  127.5 9.0 %collective-permute-start = (f32[8,128,128]{2,1,0:T(8,128)}, f32[8,128,128]{2,1,0:T(8,128)S(1)}, u32[]{:S(2)}, u32[]{:S(2)}) collective-permute-start(f32[8,128,128]{2,1,0:T(8,128)} %multiply_add_fusion.6), channel_id=1, source_target_pairs={{0,4},{4,8},{8,12},{12,16},{16,20},{20,24},{24,28},{1,5},{5,9},{9,... | collective-permute-start | bytes 1572872 | tf_op jit(solution)/shard_map/while/body/eval_jaxpr/ppermute | solution.py:15
  139.1 9.0 %collective-permute-start = (f32[8,128,128]{2,1,0:T(8,128)}, f32[8,128,128]{2,1,0:T(8,128)S(1)}, u32[]{:S(2)}, u32[]{:S(2)}) collective-permute-start(f32[8,128,128]{2,1,0:T(8,128)} %multiply_add_fusion.6), channel_id=1, source_target_pairs={{0,4},{4,8},{8,12},{12,16},{16,20},{20,24},{24,28},{1,5},{5,9},{9,... | collective-permute-start | bytes 1572872 | tf_op jit(solution)/shard_map/while/body/eval_jaxpr/ppermute | solution.py:15
  150.0 6.0 multiply_reduce_fusion.1
  156.0 2.9 copy.119
  159.0 5.0 multiply_convert_fusion.4
  166.7 40.0 %all-gather.9.cloned.1.call-done = bf16[512,1024]{1,0:T(8,128)(2,1)} async-done(((bf16[128,1024]{1,0:T(8,128)(2,1)}), bf16[512,1024]{1,0:T(8,128)(2,1)}) %all-gather.9.cloned.1.call-update) | async-done | bytes 1048592 | tf_op jit(solution)/shard_map/all_gather | solution.py:153
  206.7 3.9 fusion.100
  212.6 23.0 %all-gather.11.cloned.1.call-done = bf16[512,1024]{1,0:T(8,128)(2,1)} async-done(((bf16[128,1024]{1,0:T(8,128)(2,1)}), bf16[512,1024]{1,0:T(8,128)(2,1)}) %all-gather.11.cloned.1.call-update) | async-done | bytes 1048592 | tf_op jit(solution)/shard_map/all_gather | solution.py:161
  235.6 4.5 multiply_convert_fusion.7
  244.5 43.1 %reduce-scatter.5.cloned.1.call-done = f32[128,1024]{1,0:T(8,128)} async-done(((f32[512,1024]{1,0:T(8,128)}), f32[128,1024]{1,0:T(8,128)}) %reduce-scatter.5.cloned.1.call-update) | async-done | bytes 524304 | tf_op jit(solution)/shard_map/reduce_scatter | solution.py:168
  292.4 3.6 convolution_convert_fusion.8
  296.2 3.7 convolution_convert_fusion.6
  304.0 14.1 %all-gather.13.cloned.1.call-done = bf16[512,1024]{1,0:T(8,128)(2,1)} async-done(((bf16[128,1024]{1,0:T(8,128)(2,1)}), bf16[512,1024]{1,0:T(8,128)(2,1)}) %all-gather.13.cloned.1.call-update) | async-done | bytes 1048592 | tf_op jit(solution)/shard_map/all_gather | solution.py:176
  318.2 6.1 multiply_reduce_fusion
  328.7 2.6 multiply_convert_fusion
  332.4 4.0 while.53
  336.4 68.0 %while.54 = (s32[]{:T(128)}, f32[8,128,128]{2,1,0:T(8,128)}, f32[8]{0:T(128)S(1)}, f32[8,128,128]{2,1,0:T(8,128)S(1)}, s32[]{:T(128)}, /*index=5*/s32[]{:T(128)}) while((s32[]{:T(128)}, f32[8,128,128]{2,1,0:T(8,128)}, f32[8]{0:T(128)S(1)}, f32[8,128,128]{2,1,0:T(8,128)S(1)}, s32[]{:T(128)}, /*index=5*/s32[]{:T(128)}) %tuple.131), condition=%wide.region_20.21_spmd.clone, body=%wide.region_19.20_spmd.clone.sunk | while | flops 655363 | bytes 3145879 | solution.py:214
  344.9 5.8 collective-permute-done.1
  354.6 6.6 collective-permute-done.1
  365.2 6.6 collective-permute-done.1
  375.8 6.6 collective-permute-done.1
  386.4 6.6 collective-permute-done.1
  397.0 6.6 collective-permute-done.1
  404.5 4.1 fusion.11
  416.8 2.6 convolution_convert_fusion
  420.6 2.7 convolution_convert_fusion.3
  423.4 2.7 convolution_convert_fusion.2
  426.1 2.7 convolution_convert_fusion.1
  429.1 2.7 fusion.32
  436.8 2.7 convolution_convert_fusion.4
  440.6 2.7 fusion.106
  452.7 159.0 %all-reduce.4.cloned.1.call-done = (bf16[1024,1024]{1,0:T(8,128)(2,1)}, bf16[1024,1024]{1,0:T(8,128)(2,1)}, bf16[1024,1024]{1,0:T(8,128)(2,1)}, bf16[1024,1024]{...) async-done(((bf16[1024,1024]{1,0:T(8,128)(2,1)}, bf16[1024,1024]{1,0:T(8,128)(2,1)}, ...) | async-done | bytes 12714000 | tf_op jit(solution)/shard_map/psum | solution.py:242
  611.7 4.2 convert_element_type.180
  620.9 2.7 convert_element_type.186
  629.4 74.7 %all-gather.15.cloned.1.call-done = bf16[8192,1024]{1,0:T(8,128)(2,1)} async-done(((bf16[1024,1024]{1,0:T(8,128)(2,1)}), bf16[8192,1024]{1,0:T(8,128)(2,1)}) %all-gather.15.cloned.1.call-update) | async-done | bytes 16777232 | tf_op jit(solution)/shard_map/all_gather | solution.py:237
  704.1 10.8 %reduce_sum.94 = bf16[1024,1024]{1,0:T(8,128)(2,1)} reduce(bf16[8,1024,1024]{2,1,0:T(8,128)(2,1)} %bitcast.227, bf16[]{:T(256)} %constant.110.clone.1), dimensions={0}, to_apply=%region_22.23 | reduce | flops 7340032 | bytes 18874370 | tf_op jit(solution)/shard_map/reduce_sum | solution.py:236
  714.9 4.1 convert_element_type.178
  (319 shorter events, 139.0 us)
Async XLA Ops:
  7.2 151.8 %copy-start = (bf16[1024,1024]{1,0:T(8,128)(2,1)S(1)}, bf16[1024,1024]{1,0:T(8,128)(2,1)}, u32[]{:S(2)}) copy-start(bf16[1024,1024]{1,0:T(8,128)(2,1)} %param.28) | copy-start | bytes 6291460
  7.2 33.1 %all-gather.7.cloned.1.call-start = ((), (), s32[]{:S(2)}) async-start(), calls=%async_computation.2 | async-start | bytes 1310720 | tf_op jit(solution)/shard_map/all_gather | solution.py:94
  7.9 198.7 %all-gather.9.cloned.1.call-start = ((), (), s32[]{:S(2)}) async-start(), calls=%async_computation.3 | async-start | bytes 1310720 | tf_op jit(solution)/shard_map/all_gather | solution.py:153
  10.1 35.0 %copy-start.58 = (f32[8,2,2]{0,1,2:T(2,128)}, f32[8,2,2]{0,1,2:T(2,128)S(1)}, u32[]{:S(2)}) copy-start(f32[8,2,2]{0,1,2:T(2,128)S(1)} %copy.112) | copy-start | bytes 388
  11.5 138.5 %copy-start.69 = (f32[2]{0:T(128)}, f32[2]{0:T(128)S(1)}, u32[]{:S(2)}) copy-start(f32[2]{0:T(128)S(1)} %fusion.84) | copy-start | bytes 28
  11.6 59.5 %copy-start.56 = (f32[2,8,256]{2,1,0:T(8,128)}, f32[2,8,256]{2,1,0:T(8,128)S(1)}, u32[]{:S(2)}) copy-start(f32[2,8,256]{2,1,0:T(8,128)S(1)} %bitcast_bitcast_fusion.1) | copy-start | bytes 49156
  11.7 33.3 %copy-start.63 = (f32[2,8]{1,0:T(2,128)}, f32[2,8]{1,0:T(2,128)S(1)}, u32[]{:S(2)}) copy-start(f32[2,8]{1,0:T(2,128)S(1)} %slice_reduce_fusion) | copy-start | bytes 196
  12.4 137.6 %copy-start.64 = (f32[2,8]{1,0:T(2,128)}, f32[2,8]{1,0:T(2,128)S(1)}, u32[]{:S(2)}) copy-start(f32[2,8]{1,0:T(2,128)S(1)} %reduce_window.14) | copy-start | bytes 196
  12.4 41.6 %copy-start.61 = (f32[512]{0:T(512)}, f32[512]{0:T(512)S(1)}, u32[]{:S(2)}) copy-start(f32[512]{0:T(512)S(1)} %fusion.81) | copy-start | bytes 6148
  41.8 117.1 %copy-start.73 = (f32[512]{0:T(512)}, f32[512]{0:T(512)S(1)}, u32[]{:S(2)}) copy-start(f32[512]{0:T(512)S(1)} %add_rsqrt_fusion) | copy-start | bytes 6148
  58.9 4.6 copy-start.10
  68.7 5.5 copy-start.71
  77.3 3.0 collective-permute-start
  81.3 10.5 %collective-permute-start = (f32[8,128,128]{2,1,0:T(8,128)}, f32[8,128,128]{2,1,0:T(8,128)S(1)}, u32[]{:S(2)}, u32[]{:S(2)}) collective-permute-start(f32[8,128,128]{2,1,0:T(8,128)} %multiply_add_fusion.6), channel_id=1, source_target_pairs={{0,4},{4,8},{8,12},{12,16},{16,20},{20,24},{24,28},{1,5},{5,9},{9,... | collective-permute-start | bytes 1572872 | tf_op jit(solution)/shard_map/while/body/eval_jaxpr/ppermute | solution.py:15
  92.7 10.7 %collective-permute-start = (f32[8,128,128]{2,1,0:T(8,128)}, f32[8,128,128]{2,1,0:T(8,128)S(1)}, u32[]{:S(2)}, u32[]{:S(2)}) collective-permute-start(f32[8,128,128]{2,1,0:T(8,128)} %multiply_add_fusion.6), channel_id=1, source_target_pairs={{0,4},{4,8},{8,12},{12,16},{16,20},{20,24},{24,28},{1,5},{5,9},{9,... | collective-permute-start | bytes 1572872 | tf_op jit(solution)/shard_map/while/body/eval_jaxpr/ppermute | solution.py:15
  104.3 10.7 %collective-permute-start = (f32[8,128,128]{2,1,0:T(8,128)}, f32[8,128,128]{2,1,0:T(8,128)S(1)}, u32[]{:S(2)}, u32[]{:S(2)}) collective-permute-start(f32[8,128,128]{2,1,0:T(8,128)} %multiply_add_fusion.6), channel_id=1, source_target_pairs={{0,4},{4,8},{8,12},{12,16},{16,20},{20,24},{24,28},{1,5},{5,9},{9,... | collective-permute-start | bytes 1572872 | tf_op jit(solution)/shard_map/while/body/eval_jaxpr/ppermute | solution.py:15
  115.9 10.7 %collective-permute-start = (f32[8,128,128]{2,1,0:T(8,128)}, f32[8,128,128]{2,1,0:T(8,128)S(1)}, u32[]{:S(2)}, u32[]{:S(2)}) collective-permute-start(f32[8,128,128]{2,1,0:T(8,128)} %multiply_add_fusion.6), channel_id=1, source_target_pairs={{0,4},{4,8},{8,12},{12,16},{16,20},{20,24},{24,28},{1,5},{5,9},{9,... | collective-permute-start | bytes 1572872 | tf_op jit(solution)/shard_map/while/body/eval_jaxpr/ppermute | solution.py:15
  127.5 10.7 %collective-permute-start = (f32[8,128,128]{2,1,0:T(8,128)}, f32[8,128,128]{2,1,0:T(8,128)S(1)}, u32[]{:S(2)}, u32[]{:S(2)}) collective-permute-start(f32[8,128,128]{2,1,0:T(8,128)} %multiply_add_fusion.6), channel_id=1, source_target_pairs={{0,4},{4,8},{8,12},{12,16},{16,20},{20,24},{24,28},{1,5},{5,9},{9,... | collective-permute-start | bytes 1572872 | tf_op jit(solution)/shard_map/while/body/eval_jaxpr/ppermute | solution.py:15
  139.1 10.7 %collective-permute-start = (f32[8,128,128]{2,1,0:T(8,128)}, f32[8,128,128]{2,1,0:T(8,128)S(1)}, u32[]{:S(2)}, u32[]{:S(2)}) collective-permute-start(f32[8,128,128]{2,1,0:T(8,128)} %multiply_add_fusion.6), channel_id=1, source_target_pairs={{0,4},{4,8},{8,12},{12,16},{16,20},{20,24},{24,28},{1,5},{5,9},{9,... | collective-permute-start | bytes 1572872 | tf_op jit(solution)/shard_map/while/body/eval_jaxpr/ppermute | solution.py:15
  150.0 6.0 copy-start.54
  158.9 5.1 copy-start.59
  158.9 5.1 copy-start.16
  159.0 5.1 copy-start.24
  165.0 123.8 %copy-start.6 = (f32[128,1024]{1,0:T(8,128)}, f32[128,1024]{1,0:T(8,128)S(1)}, u32[]{:S(2)}) copy-start(f32[128,1024]{1,0:T(8,128)S(1)} %get-tuple-element.309) | copy-start | bytes 1572868
  165.0 123.8 %copy-start.67 = (f32[128]{0:T(128)}, f32[128]{0:T(128)S(1)}, u32[]{:S(2)}) copy-start(f32[128]{0:T(128)S(1)} %add_rsqrt_fusion.2) | copy-start | bytes 1540
  165.9 69.7 %all-gather.11.cloned.1.call-start = ((), (), s32[]{:S(2)}) async-start(), calls=%async_computation.5 | async-start | bytes 1310720 | tf_op jit(solution)/shard_map/all_gather | solution.py:161
  166.6 120.9 %reduce-scatter.5.cloned.1.call-start = ((), (), s32[]{:S(2)}) async-start(), calls=%async_computation.6 | async-start | bytes 2621440 | tf_op jit(solution)/shard_map/reduce_scatter | solution.py:168
  235.6 4.5 copy-start.82
  244.4 44.4 %copy-start.30 = (bf16[128,1024]{1,0:T(8,128)(2,1)S(1)}, bf16[128,1024]{1,0:T(8,128)(2,1)}, u32[]{:S(2)}) copy-start(bf16[128,1024]{1,0:T(8,128)(2,1)} %param.33) | copy-start | bytes 786436
  244.4 46.5 %copy-start.75 = (f32[1,8]{1,0:T(1,128)S(1)}, f32[1,8]{1,0:T(1,128)}, u32[]{:S(2)}) copy-start(f32[1,8]{1,0:T(1,128)} %get-tuple-element.302) | copy-start | bytes 100
  244.4 73.7 %all-gather.13.cloned.1.call-start = ((), (), s32[]{:S(2)}) async-start(), calls=%async_computation.7 | async-start | bytes 1310720 | tf_op jit(solution)/shard_map/all_gather | solution.py:176
  290.8 159.2 %reduce-scatter.3.cloned.1.call-start = ((), (), s32[]{:S(2)}) async-start(), calls=%async_computation.4 | async-start | bytes 1310720 | tf_op jit(solution)/shard_map/reduce_scatter | solution.py:157
  296.0 315.7 %all-reduce.4.cloned.1.call-start = ((), (), s32[]{:S(2)}) async-start(), calls=%async_computation.9 | async-start | bytes 25427968 | tf_op jit(solution)/shard_map/psum | solution.py:242
  302.0 16.2 %copy-start.60 = (f32[1,2,2,128]{3,1,2,0:T(2,128)S(1)}, f32[1,2,2,128]{3,1,2,0:T(2,128)}, u32[]{:S(2)}) copy-start(f32[1,2,2,128]{3,1,2,0:T(2,128)} %copy-done.59) | copy-start | bytes 6148
  318.2 6.1 copy-start.2
  325.1 6.2 copy-start.3
  336.4 68.0 %copy-start.66 = (f32[2,8]{1,0:T(2,128)S(1)}, f32[2,8]{1,0:T(2,128)}, u32[]{:S(2)}) copy-start(f32[2,8]{1,0:T(2,128)} %rev.8) | copy-start | bytes 196
  337.3 3.6 collective-permute-start.1
  343.6 7.0 collective-permute-start.1
  353.4 7.9 %collective-permute-start.1 = (bf16[8,128,128]{2,1,0:T(8,128)(2,1)}, bf16[8,128,128]{2,1,0:T(8,128)(2,1)S(1)}, u32[]{:S(2)}, u32[]{:S(2)}) collective-permute-start(bf16[8,128,128]{2,1,0:T(8,128)(2,1)} %fusion.155), channel_id=1, source_target_pairs={{4,0},{8,4},{12,8},{16,12},{20,16},{24,20},{28,24},{5,1},{9,5},{13... | collective-permute-start | bytes 786440 | tf_op jit(solution)/shard_map/while/body/eval_jaxpr/ppermute | solution.py:15
  363.9 7.9 %collective-permute-start.1 = (bf16[8,128,128]{2,1,0:T(8,128)(2,1)}, bf16[8,128,128]{2,1,0:T(8,128)(2,1)S(1)}, u32[]{:S(2)}, u32[]{:S(2)}) collective-permute-start(bf16[8,128,128]{2,1,0:T(8,128)(2,1)} %fusion.155), channel_id=1, source_target_pairs={{4,0},{8,4},{12,8},{16,12},{20,16},{24,20},{28,24},{5,1},{9,5},{13... | collective-permute-start | bytes 786440 | tf_op jit(solution)/shard_map/while/body/eval_jaxpr/ppermute | solution.py:15
  374.5 7.9 %collective-permute-start.1 = (bf16[8,128,128]{2,1,0:T(8,128)(2,1)}, bf16[8,128,128]{2,1,0:T(8,128)(2,1)S(1)}, u32[]{:S(2)}, u32[]{:S(2)}) collective-permute-start(bf16[8,128,128]{2,1,0:T(8,128)(2,1)} %fusion.155), channel_id=1, source_target_pairs={{4,0},{8,4},{12,8},{16,12},{20,16},{24,20},{28,24},{5,1},{9,5},{13... | collective-permute-start | bytes 786440 | tf_op jit(solution)/shard_map/while/body/eval_jaxpr/ppermute | solution.py:15
  385.1 7.9 %collective-permute-start.1 = (bf16[8,128,128]{2,1,0:T(8,128)(2,1)}, bf16[8,128,128]{2,1,0:T(8,128)(2,1)S(1)}, u32[]{:S(2)}, u32[]{:S(2)}) collective-permute-start(bf16[8,128,128]{2,1,0:T(8,128)(2,1)} %fusion.155), channel_id=1, source_target_pairs={{4,0},{8,4},{12,8},{16,12},{20,16},{24,20},{28,24},{5,1},{9,5},{13... | collective-permute-start | bytes 786440 | tf_op jit(solution)/shard_map/while/body/eval_jaxpr/ppermute | solution.py:15
  395.7 7.9 %collective-permute-start.1 = (bf16[8,128,128]{2,1,0:T(8,128)(2,1)}, bf16[8,128,128]{2,1,0:T(8,128)(2,1)S(1)}, u32[]{:S(2)}, u32[]{:S(2)}) collective-permute-start(bf16[8,128,128]{2,1,0:T(8,128)(2,1)} %fusion.155), channel_id=1, source_target_pairs={{4,0},{8,4},{12,8},{16,12},{20,16},{24,20},{28,24},{5,1},{9,5},{13... | collective-permute-start | bytes 786440 | tf_op jit(solution)/shard_map/while/body/eval_jaxpr/ppermute | solution.py:15
  404.5 4.1 copy-start.20
  411.1 12.3 %copy-start.50 = (bf16[2,256,8,128]{3,2,1,0:T(8,128)(2,1)}, bf16[2,256,8,128]{3,2,1,0:T(8,128)(2,1)S(1)}, u32[]{:S(2)}) copy-start(bf16[2,256,8,128]{3,2,1,0:T(8,128)(2,1)S(1)} %copy.126) | copy-start | bytes 3145732
  428.8 275.3 %all-gather.15.cloned.1.call-start = ((), (), s32[]{:S(2)}) async-start(), calls=%async_computation.8 | async-start | bytes 18874368 | tf_op jit(solution)/shard_map/all_gather | solution.py:237
  611.7 4.2 copy-start.33
  (61 other events, 130.8 us)
Sparse Core Ops, SparseCore 0:
  9.6 30.6 all-gather.6
  166.0 40.5 all-gather.8
  208.2 27.3 all-gather.10
  244.6 42.9 reduce-scatter.4
  290.9 27.1 all-gather.12
  320.3 26.6 reduce-scatter.2
  428.9 182.7 all-reduce.3
  614.1 89.8 all-gather.14
